TPU v7x, 128 devices: a whole 4x4x4 slice. The times are simulated.
128 devices in a mesh: sub: 8 (over z, core), grp: 16 (over x, y).
Axes of the slice: x: 4, y: 4, z: 4, core: 2. Of those that a mesh axis runs over, the one named last changes fastest.
Arguments:
- schur: bfloat16 [512, 1024, 1024], P(('sub', 'grp')), as said below
- mortar: bfloat16 [512, 8, 128, 128], P(('sub', 'grp')), may hold values from -0.5 to 0.5
- partner: int32 [512, 4], P(('sub', 'grp')), may hold values from 0 to 15, as said below
- corner_map: int32 [512, 8], P(('sub', 'grp')), may hold values from 0 to 127
- coarse_inv: float32 [8, 128, 128], P('sub'), as said below
- load: float32 [512, 1024, 384], P(('sub', 'grp')), may hold values from -6 to 6
Outputs:
- solution: float32 [512, 1024, 384], P(('sub', 'grp'))
Inputs may be any that keep to these rules, and one draw needn't show every extreme that they name: `partner`: within the 4 subdomains of one device, the entries form a permutation of 0 to 15. `schur`: each matrix is symmetric positive definite. `coarse_inv`: each matrix is symmetric positive definite.
All inputs are finite; a program needn't handle non-finite values.
Results may differ from a plain program's by a relative error of at most 0.0025.
Values may be sent and summed in bfloat16 or wider, within the bound.
A program may use at most 128 MiB of HBM per device.

v0:
```python
import jax
import jax.numpy as jnp
from jax import lax
from jax.sharding import PartitionSpec as P

ITERS = 2


def shifted(block, axis, distance):
    devices = range(lax.axis_size(axis))
    route = [((i - distance) % len(devices), i) for i in devices]
    return lax.ppermute(block, axis, route)


def face_terms(direction, schur, mortar, partner):
    subdoms = direction.shape[0]
    order = direction.shape[1]
    columns = direction.shape[2]
    faces_all = mortar.shape[1]
    block = mortar.shape[2]
    half_faces = faces_all // 2
    dir_half = direction.astype(jnp.bfloat16)
    stiff = jnp.einsum("sij,sjr->sir", schur, dir_half, preferred_element_type=jnp.float32)
    face_rows = dir_half.reshape(subdoms, faces_all, block, columns)
    traces = jnp.einsum(
        "sfij,sfjr->sfir", mortar, face_rows, preferred_element_type=jnp.float32
    ).astype(jnp.bfloat16)
    upper = traces[:, :half_faces].reshape(subdoms * half_faces, block, columns)
    lower = traces[:, half_faces:].reshape(subdoms * half_faces, block, columns)
    mates = partner.reshape(-1)
    inverse = jnp.argsort(mates)
    reordered = jnp.take(upper, inverse, axis=0)
    lower_mate = shifted(reordered, "sub", 1)
    jump_lower = (lower.astype(jnp.float32) - lower_mate.astype(jnp.float32)).astype(jnp.bfloat16)
    above = shifted(lower, "sub", -1)
    upper_mate = jnp.take(above, mates, axis=0)
    jump_upper = (upper.astype(jnp.float32) - upper_mate.astype(jnp.float32)).astype(jnp.bfloat16)
    jump_all = jnp.concatenate(
        [
            jump_upper.reshape(subdoms, half_faces, block, columns),
            jump_lower.reshape(subdoms, half_faces, block, columns),
        ],
        axis=1,
    )
    pulled = jnp.einsum("sfji,sfjr->sfir", mortar, jump_all, preferred_element_type=jnp.float32)
    return stiff + pulled.reshape(subdoms, order, columns)


def squares(residual):
    return lax.psum(jnp.sum(residual * residual, axis=(0, 1)), ("sub", "grp"))


def on_device(schur, mortar, partner, corner_map, coarse_inv, load):
    order = load.shape[1]
    corner_count = corner_map.shape[1]
    coarse_count = coarse_inv.shape[1]
    stride = order // corner_count
    onehot = (corner_map[..., None] == jnp.arange(coarse_count, dtype=jnp.int32)).astype(
        jnp.float32
    )
    coarse_matrix = coarse_inv[0]
    solution = jnp.zeros_like(load)
    residual = load
    direction = load
    norm_now = squares(residual)
    for step in range(ITERS):
        partial_value = face_terms(direction, schur, mortar, partner)
        corners = direction[:, ::stride, :]
        local_sum = jnp.einsum("sco,scr->or", onehot, corners, precision=lax.Precision.HIGHEST)
        coarse_sum = lax.psum(local_sum.astype(jnp.bfloat16), "grp").astype(jnp.float32)
        coarse_val = jnp.dot(coarse_matrix, coarse_sum, precision=lax.Precision.HIGHEST)
        corner_add = jnp.einsum("sco,or->scr", onehot, coarse_val, precision=lax.Precision.HIGHEST)
        image = partial_value.at[:, ::stride, :].add(corner_add)
        curvature = lax.psum(jnp.sum(direction * image, axis=(0, 1)), ("sub", "grp"))
        image, curvature = (image, curvature)
        step_len = norm_now / curvature
        solution = solution + step_len * direction
        if step + 1 < ITERS:
            residual = residual - step_len * image
            norm_next = squares(residual)
            direction = residual + norm_next / norm_now * direction
            norm_now = norm_next
    return solution


def solution(mesh):
    return jax.shard_map(
        on_device,
        mesh=mesh,
        in_specs=(
            P(("sub", "grp"), None, None),
            P(("sub", "grp"), None, None, None),
            P(("sub", "grp"), None),
            P(("sub", "grp"), None),
            P("sub", None, None),
            P(("sub", "grp"), None, None),
        ),
        out_specs=P(("sub", "grp"), None, None),
        check_vma=False,
    )
```

profile of v0, /device:TPU:1, one launch (start us, length us, event | category | flops | bytes accessed | tf_op | source)
XLA Modules:
  0.0 520.1 jit_solution(5917532602240920158)
XLA Ops:
  6.5 5.6 %multiply_reduce_fusion.1 = (f32[384]{0:T(512)S(1)}, bf16[4,1024,384]{2,1,0:T(8,128)(2,1)S(1)}) fusion(f32[4,1024,384]{2,1,0:T(8,128)} %param.13), kind=kLoop, calls=%fused_computation.17 | loop fusion | flops 4718208 | bytes 9438720 | tf_op jit(solution)/shard_map/reduce_sum | solution.py:50
  20.0 2.8 broadcast_select_fusion.1
  24.4 2.8 slice.20
  28.6 82.6 %all-reduce.4.cloned.1.call-done = bf16[128,384]{1,0:T(8,128)(2,1)} async-done(((bf16[128,384]{1,0:T(8,128)(2,1)}), bf16[128,384]{1,0:T(8,128)(2,1)}) %all-reduce.4.cloned.1.call-update) | async-done | bytes 98320 | tf_op jit(solution)/shard_map/psum | solution.py:70
  112.7 3.3 gather_fusion
  123.9 6.9 %bitcast_add_fusion = f32[4,1024,384]{2,1,0:T(8,128)} fusion(f32[4,8,384,128]{2,3,1,0:T(8,128)S(1)} %fusion.3, bf16[4,1024,1024]{2,1,0:T(8,128)(2,1)S(1)} %bitcast.65, bf16[4,1024,384]{2,1,0:T(8,128)(2,1)S(1)} %copy-done.2), kind=kOutput, calls=%fused_computation.6 | convolution fusion | flops 3222798336 | bytes 24117248 | tf_op jit(solution)/shard_map/sij,sjr->sir/dot_general | solution.py:23
  130.8 9.5 %copy.24 = f32[4,1024,384]{2,0,1:T(4,128)} copy(f32[4,1024,384]{2,1,0:T(8,128)} %bitcast_add_fusion) | data formatting | bytes 12582912 | tf_op jit(solution)/shard_map/add | solution.py:46
  142.4 9.6 %fusion.2 = f32[384]{0:T(512)S(1)} fusion(f32[4,1024,384]{2,0,1:T(4,128)} %scatter_fusion, f32[4,1024,384]{2,1,0:T(8,128)} %param.13), kind=kLoop, calls=%fused_computation.13 | loop fusion | flops 3145344 | bytes 12584448 | tf_op jit(solution)/shard_map/reduce_sum | solution.py:74
  152.0 64.9 %all-reduce = (f32[384]{0:T(512)S(1)}, f32[384]{0:T(512)S(1)}) all-reduce(f32[384]{0:T(512)S(1)} %get-tuple-element.12, f32[384]{0:T(512)S(1)} %fusion.2), channel_id=1, replica_groups=mesh['sub'=8,'grp'=16] {'sub','grp'}, use_global_device_ids=true, to_apply=%region_1.0 | all-reduce | flops 768 | bytes 6144 | tf_op jit(solution)/shard_map/psum | solution.py:50
  216.9 5.5 %multiply_reduce_fusion = f32[384]{0:T(512)S(1)} fusion(f32[4,1024,384]{2,1,0:T(8,128)} %param.13, f32[4,1024,384]{2,0,1:T(4,128)} %scatter_fusion, f32[384]{0:T(512)S(1)} %div.9), kind=kLoop, calls=%fused_computation.16 | loop fusion | flops 6291072 | bytes 12585984 | tf_op jit(solution)/shard_map/reduce_sum | solution.py:50
  222.4 64.4 %psum.45 = f32[384]{0:T(512)S(1)} all-reduce(f32[384]{0:T(512)S(1)} %multiply_reduce_fusion), channel_id=1, replica_groups=mesh['sub'=8,'grp'=16] {'sub','grp'}, use_global_device_ids=true, to_apply=%region_8.10 | all-reduce | flops 384 | bytes 3072 | tf_op jit(solution)/shard_map/psum | solution.py:50
  286.8 7.1 %fusion.21 = (bf16[4,1024,384]{2,1,0:T(8,128)(2,1)S(1)}, f32[4,1024,384]{2,1,0:T(8,128)}) fusion(f32[4,1024,384]{2,1,0:T(8,128)} %param.13, f32[384]{0:T(512)S(1)} %div.10, f32[4,1024,384]{2,0,1:T(4,128)} %scatter_fusion, f32[384]{0:T(512)S(1)} %div.9), kind=kLoop, calls=%fused_computation.58 | loop fusion | flops 7864320 | bytes 22023168 | tf_op jit(solution)/shard_map/convert_element_type | solution.py:22
  302.7 2.8 slice.23
  306.5 78.2 %all-reduce.6.cloned.1.call-done = bf16[128,384]{1,0:T(8,128)(2,1)} async-done(((bf16[128,384]{1,0:T(8,128)(2,1)}), bf16[128,384]{1,0:T(8,128)(2,1)}) %all-reduce.6.cloned.1.call-update) | async-done | bytes 98320 | tf_op jit(solution)/shard_map/psum | solution.py:70
  386.1 3.5 subtract_convert_fusion
  392.2 3.3 gather_fusion.2
  395.5 3.1 subtract_convert_fusion.1
  401.3 5.1 fusion.7
  406.4 6.5 %copy.41 = f32[4,1024,384]{1,2,0:T(8,128)} copy(f32[4,1024,384]{2,1,0:T(8,128)} %bitcast.68) | data formatting | bytes 12582912 | tf_op jit(solution)/shard_map/reshape | solution.py:46
  413.0 12.4 %bitcast_add_fusion.1 = f32[4,1024,384]{1,2,0:T(8,128)} fusion(f32[4,1024,384]{1,2,0:T(8,128)} %copy.41, bf16[4,1024,384]{2,1,0:T(8,128)(2,1)} %copy-done.3, bf16[4,1024,1024]{2,1,0:T(8,128)(2,1)} %param.8), kind=kOutput, calls=%fused_computation.7 | convolution fusion | flops 3222798336 | bytes 24117248 | tf_op jit(solution)/shard_map/sij,sjr->sir/dot_general | solution.py:23
  425.3 7.7 %copy.34 = f32[4,1024,384]{2,0,1:T(4,128)} copy(f32[4,1024,384]{1,2,0:T(8,128)} %bitcast_add_fusion.1) | data formatting | bytes 12582912 | tf_op jit(solution)/shard_map/add | solution.py:46
  435.1 5.3 %fusion = f32[384]{0:T(512)S(1)} fusion(f32[4,1024,384]{2,1,0:T(8,128)} %get-tuple-element.11, f32[4,1024,384]{2,0,1:T(4,128)} %scatter_fusion.1), kind=kLoop, calls=%fused_computation.9 | loop fusion | flops 3145344 | bytes 12584448 | tf_op jit(solution)/shard_map/reduce_sum | solution.py:74
  440.3 64.9 %psum.47 = f32[384]{0:T(512)S(1)} all-reduce(f32[384]{0:T(512)S(1)} %fusion), channel_id=1, replica_groups=mesh['sub'=8,'grp'=16] {'sub','grp'}, use_global_device_ids=true, to_apply=%region_12.14 | all-reduce | flops 384 | bytes 3072 | tf_op jit(solution)/shard_map/psum | solution.py:74
  505.2 8.0 %multiply_add_fusion = f32[4,1024,384]{2,1,0:T(8,128)} fusion(f32[4,1024,384]{2,1,0:T(8,128)} %get-tuple-element.11, f32[4,1024,384]{2,1,0:T(8,128)} %param.13, f32[384]{0:T(512)S(1)} %div.11, f32[384]{0:T(512)S(1)} %div.9), kind=kLoop, calls=%fused_computation.14 | loop fusion | flops 4718592 | bytes 18877440 | tf_op jit(solution)/shard_map/add | solution.py:77
  (68 shorter events, 40.6 us)
Async XLA Ops:
  6.5 5.6 %copy-start = (bf16[4,8,128,128]{3,2,1,0:T(8,128)(2,1)S(1)}, bf16[4,8,128,128]{3,2,1,0:T(8,128)(2,1)}, u32[]{:S(2)}) copy-start(bf16[4,8,128,128]{3,2,1,0:T(8,128)(2,1)} %param.9) | copy-start | bytes 3145732
  6.5 104.7 %all-reduce.4.cloned.1.call-start = ((), (), s32[]{:S(2)}) async-start(), calls=%async_computation | async-start | bytes 196608 | tf_op jit(solution)/shard_map/psum | solution.py:70
  12.2 1.7 copy-start.1
  13.8 3.0 copy-start.7
  15.4 97.3 %collective-permute-start = (bf16[16,128,384]{2,1,0:T(8,128)(2,1)}, bf16[16,128,384]{2,1,0:T(8,128)(2,1)}, u32[]{:S(2)}, u32[]{:S(2)}) collective-permute-start(bf16[16,128,384]{2,1,0:T(8,128)(2,1)} %bitcast.2), channel_id=1, source_target_pairs={{16,0},{32,16},{48,32},{64,48},{80,64},{96,80},{112,96},{0,112},{1... | collective-permute-start | bytes 4718600 | tf_op jit(solution)/shard_map/ppermute | solution.py:12
  18.1 9.2 %copy-start.6 = (s32[4,8]{1,0:T(4,128)S(1)}, s32[4,8]{1,0:T(4,128)}, u32[]{:S(2)}) copy-start(s32[4,8]{1,0:T(4,128)} %param.11) | copy-start | bytes 388
  18.1 93.1 %copy-start.5 = (f32[1,128,128]{2,1,0:T(8,128)S(1)}, f32[1,128,128]{2,1,0:T(8,128)}, u32[]{:S(2)}) copy-start(f32[1,128,128]{2,1,0:T(8,128)} %param.12) | copy-start | bytes 196612
  22.8 95.3 %collective-permute-start.1 = (bf16[16,128,384]{2,1,0:T(8,128)(2,1)}, bf16[16,128,384]{2,1,0:T(8,128)(2,1)}, u32[]{:S(2)}, u32[]{:S(2)}) collective-permute-start(bf16[16,128,384]{2,1,0:T(8,128)(2,1)} %broadcast_select_fusion.1), channel_id=1, source_target_pairs={{112,0},{0,16},{16,32},{32,48},{48,64},{64,80},{80,96},{96,112},{1... | collective-permute-start | bytes 4718600 | tf_op jit(solution)/shard_map/ppermute | solution.py:12
  28.3 356.4 %all-reduce.6.cloned.1.call-start = ((), (), s32[]{:S(2)}) async-start(), calls=%async_computation.1 | async-start | bytes 196608 | tf_op jit(solution)/shard_map/psum | solution.py:70
  118.2 3.6 slice-start
  120.7 2.3 slice-start.1
  120.7 3.2 copy-start.2
  293.9 1.7 copy-start.3
  301.7 84.4 %collective-permute-start.3 = (bf16[16,128,384]{1,2,0:T(8,128)(2,1)}, bf16[16,128,384]{1,2,0:T(8,128)(2,1)}, u32[]{:S(2)}, u32[]{:S(2)}) collective-permute-start(bf16[16,128,384]{1,2,0:T(8,128)(2,1)} %broadcast_select_fusion), channel_id=1, source_target_pairs={{112,0},{0,16},{16,32},{32,48},{48,64},{64,80},{80,96},{96,112},{1... | collective-permute-start | bytes 4718600 | tf_op jit(solution)/shard_map/ppermute | solution.py:12
  301.7 90.5 %collective-permute-start.2 = (bf16[16,128,384]{1,2,0:T(8,128)(2,1)}, bf16[16,128,384]{1,2,0:T(8,128)(2,1)}, u32[]{:S(2)}, u32[]{:S(2)}) collective-permute-start(bf16[16,128,384]{1,2,0:T(8,128)(2,1)} %bitcast.16), channel_id=1, source_target_pairs={{16,0},{32,16},{48,32},{64,48},{80,64},{96,80},{112,96},{0,112},{1... | collective-permute-start | bytes 4718600 | tf_op jit(solution)/shard_map/ppermute | solution.py:12
  398.7 2.7 copy-start.4
Sparse Core Ops, SparseCore 0:
  28.4 82.7 all-reduce.3
  306.6 77.9 all-reduce.5
where the time goes:
time: 521 us; the launch traced here: 520 us
  blocking collectives  194 us (37%)
  waiting for transfers between devices  161 us (31%)
  other arithmetic  63.4 us (12%)
  local copies, waits for them, and re-layouts  51.5 us (10%)
  matrix products  32.3 us (6%)
  between operations  13.6 us (3%)
    psum x2, waiting for transfers between devices, on_device(): lax.psum(local_sum.astype(jnp.bfloat16), 'grp').astype(jnp.float32)  161 us
    psum x2, blocking collectives, squares(): return lax.psum(jnp.sum(residual * residual, axis=(0, 1)), ('sub', 'grp'))  129 us
    psum x1, blocking collectives, on_device(): lax.psum(jnp.sum(direction * image, axis=(0, 1)), ('sub', 'grp'))  64.9 us
    dot_general x2, matrix products, face_terms(): jnp.einsum('sij,sjr->sir', schur, dir_half, preferred_element_type=jnp.fl...  19.3 us
    add x2, local copies, waits for them, and re-layouts, face_terms(): return stiff + pulled.reshape(subdoms, order, columns)  17.1 us
    reduce_sum x2, other arithmetic, on_device(): jnp.sum(direction * image, axis=(0, 1))  14.9 us
    reduce_sum x2, other arithmetic, squares(): return lax.psum(jnp.sum(residual * residual, axis=(0, 1)), ('sub', 'grp'))  11.1 us
  transfers between devices with their start and end apart: 6, of which 2 were waited for; matrix products, arithmetic and copies ran while one was open for 5% of the time, Pallas kernels for 0%

commit v1 on v0

v1 whole, which is shorter than its diff:
```python
import functools

import jax
import jax.numpy as jnp
from jax import lax
from jax.experimental import pallas as pl
from jax.experimental.pallas import tpu as pltpu
from jax.sharding import PartitionSpec as P

F32, BF16 = jnp.float32, jnp.bfloat16
SUBDOMS, HALF, FACES = 4, 4, 8
BLOCK, COLS, ORDER = 128, 384, 1024
ALL, SLOTS, COARSE = 32, 16, 128
SIDE = 4
N_SUB = 8
N_GRP = 16
UP = 7
MESH = pl.DeviceIdType.MESH
EXACT = lax.Precision.HIGHEST


def low(s, k):
    return s * FACES + HALF + k


def rows8(a):
    return jnp.sum(a.reshape(BLOCK // 8, 8, COLS), axis=0)


def one_row(acc):
    return jnp.sum(acc, axis=0, keepdims=True)


def mul(a, b):
    return jnp.dot(a, b, preferred_element_type=F32)


def mul_t(a, b):
    return lax.dot_general(a, b, (((0,), (0,)), ((), ())), preferred_element_type=F32)


def kernel(
    schur_h, mortar_h, load_h, coarse_h, partner, cmap, out_h,
    S, M, B, K, VB, Q, RB, TR, SU, AB, MT, JU, TQ, SU2, RU2, RD2,
    OH, CR, CX, RX, CY, RY, GY, GX, CA, RS, AS, AX, AY, AZ, INV,
    load_s, mort_s, schur_s, coarse_s, out_s,
    sd_s, sd_r, su_s, su_r, td_s, td_r, tu_s, tu_r,
    g_s, g_r, z_s, z_r, f_s, f_r,
):
    sub, grp = lax.axis_index("sub"), lax.axis_index("grp")
    gx, gy = grp // SIDE, grp % SIDE
    above, below = (sub + 1) % N_SUB, (sub + N_SUB - 1) % N_SUB

    def along_x(d):
        return {"grp": ((gx + d) % SIDE) * SIDE + gy}

    def along_y(d):
        return {"grp": gx * SIDE + (gy + d) % SIDE}

    def along_sub(d):
        return {"sub": (sub + d) % N_SUB}

    def send(src, dst, ssem, rsem, device):
        return pltpu.make_async_remote_copy(
            src_ref=src, dst_ref=dst, send_sem=ssem, recv_sem=rsem,
            device_id=device, device_id_type=MESH,
        )

    def send_down(j):
        s, k = j // HALF, j % HALF
        return send(TR.at[low(s, k)], AB.at[j], sd_s.at[j], sd_r.at[j], {"sub": below})

    def send_up(j):
        return send(SU.at[j], MT.at[j], su_s.at[j], su_r.at[j], {"sub": above})

    def send_up2(j):
        return send(SU2.at[j], RU2.at[j], tu_s.at[j], tu_r.at[j], {"sub": above})

    def send_down2(j):
        s, k = j // HALF, j % HALF
        return send(
            TQ.at[low(s, k)], RD2.at[j - UP], td_s.at[j - UP], td_r.at[j - UP], {"sub": below}
        )

    mort_c = pltpu.make_async_copy(mortar_h, M, mort_s)
    mort_c.start()

    def load_c(s):
        span = pl.ds(s * FACES, FACES)
        return pltpu.make_async_copy(load_h.at[span], B.at[span], load_s.at[s])

    def schur_c(s):
        return pltpu.make_async_copy(schur_h.at[s], S.at[s], schur_s.at[s])

    coarse_c = pltpu.make_async_copy(coarse_h.at[0], K, coarse_s)
    for s in range(SUBDOMS):
        load_c(s).start()
    coarse_c.start()
    for s in range(SUBDOMS):
        schur_c(s).start()

    barrier = pltpu.get_barrier_semaphore()
    for d in range(1, SIDE):
        pl.semaphore_signal(barrier, inc=1, device_id=along_x(d), device_id_type=MESH)
        pl.semaphore_signal(barrier, inc=1, device_id=along_y(d), device_id_type=MESH)
    for d in range(1, N_SUB):
        pl.semaphore_signal(barrier, inc=1, device_id=along_sub(d), device_id_type=MESH)

    @pl.loop(0, SLOTS)
    def _(j):
        found = jnp.int32(0)
        for u in range(SLOTS):
            at = (u // HALF) * FACES + u % HALF
            found = jnp.where(partner[u // HALF, u % HALF] == j, at, found)
        INV[j] = found

    lanes = lax.broadcasted_iota(jnp.int32, (1, COARSE), 1)

    @pl.loop(0, SUBDOMS)
    def _(s):
        for c in range(FACES):
            OH[pl.ds(s * FACES + c, 1), :] = jnp.where(lanes == cmap[s, c], 1.0, 0.0).astype(F32)

    mort_c.wait()

    def first(s, acc):
        load_c(s).wait()
        for f in range(FACES):
            g = s * FACES + f
            b = B[g]
            acc = acc + rows8(b * b)
            half = b.astype(BF16)
            VB[g] = half
            TR[g] = mul(M[g], half).astype(BF16)
        return acc

    acc0 = lax.fori_loop(0, SUBDOMS, first, jnp.zeros((8, COLS), F32))
    pl.semaphore_wait(barrier, 2 * (SIDE - 1) + N_SUB - 1)

    @pl.loop(0, SLOTS)
    def _(j):
        send_down(j).start()
        SU[j] = TR[INV[j]]
        send_up(j).start()

    def coarse_pass(p, fields, row0, row1, work):
        @pl.loop(0, ALL)
        def _(g):
            CR[pl.ds(g, 1), :] = fields[g, 0:1, :]

        local = lax.dot_general(
            OH[...], CR[...], (((0,), (0,)), ((), ())), precision=EXACT, preferred_element_type=F32
        )
        for i in range(SIDE):
            CX[p, i, 0:32, :] = local[32 * i : 32 * i + 32]
            CX[p, i, 32:33, :] = row0
            CX[p, i, 33:34, :] = row1
            CX[p, i, 34:40, :] = jnp.zeros((6, COLS), F32)

        def rs_x(d):
            return send(
                CX.at[p, (gx + d) % SIDE], RX.at[p, d - 1], g_s.at[p, 0, d - 1], g_r.at[p, 0, d - 1],
                along_x(d),
            )

        def rs_y(d):
            return send(
                CY.at[p, (gy + d) % SIDE], RY.at[p, d - 1], g_s.at[p, 1, d - 1], g_r.at[p, 1, d - 1],
                along_y(d),
            )

        def ag_y(d):
            return send(
                GY.at[p, gy], GY.at[p, gy], g_s.at[p, 2, d - 1], g_r.at[p, 2, d - 1], along_y(d)
            )

        def ag_x(d):
            return send(
                GX.at[p, gx], GX.at[p, gx], g_s.at[p, 3, d - 1], g_r.at[p, 3, d - 1], along_x(d)
            )

        dist = range(1, SIDE)
        for d in dist:
            rs_x(d).start()
        work(0)
        for d in dist:
            rs_x(d).wait_recv()
        total = CX[p, gx] + RX[p, 0] + RX[p, 1] + RX[p, 2]
        for i in range(SIDE):
            CY[p, i, 0:8, :] = total[8 * i : 8 * i + 8]
            CY[p, i, 8:16, :] = total[32:40]
        for d in dist:
            rs_y(d).start()
        work(1)
        for d in dist:
            rs_y(d).wait_recv()
        total = CY[p, gy] + RY[p, 0] + RY[p, 1] + RY[p, 2]
        GY[p, gy] = total[0:8]
        for d in dist:
            ag_y(d).start()
        work(2, total[8:16])
        for d in dist:
            ag_y(d).wait_recv()
        GX[p, gx] = GY[p].reshape(32, COLS)
        for d in dist:
            ag_x(d).start()
        work(3)
        for d in dist:
            ag_x(d).wait_recv()
        for d in dist:
            rs_x(d).wait_send()
            rs_y(d).wait_send()
            ag_y(d).wait_send()
            ag_x(d).wait_send()
        return GX[p].reshape(COARSE, COLS)

    TILE = 512

    def stiff(s, *_):
        schur_c(s).wait()
        field = VB[s * FACES : (s + 1) * FACES].reshape(ORDER, COLS)

        @pl.loop(0, ORDER // TILE)
        def _(i):
            part = mul(S[s, pl.ds(pl.multiple_of(i * TILE, TILE), TILE), :], field)
            Q[pl.ds(s * FACES + i * (TILE // BLOCK), TILE // BLOCK)] = part.reshape(
                TILE // BLOCK, BLOCK, COLS
            )

    zero = jnp.zeros((1, COLS), F32)
    coarse_c.wait()
    sum_b = coarse_pass(0, B, zero, zero, stiff)
    coarse_val = jnp.dot(K[...], sum_b, precision=EXACT, preferred_element_type=F32)
    CA[...] = jnp.dot(OH[...], coarse_val, precision=EXACT, preferred_element_type=F32)

    def finish(g, mate, acc):
        jump = (TR[g].astype(F32) - mate.astype(F32)).astype(BF16)
        JU[g] = jump
        Q[g] = Q[g] + mul_t(M[g], jump)
        Q[g, 0:1, :] = Q[g, 0:1, :] + CA[pl.ds(g, 1), :]
        q = Q[g]
        TQ[g] = mul(M[g], q.astype(BF16)).astype(BF16)
        return acc + rows8(B[g] * q)

    @pl.loop(0, SLOTS)
    def _(j):
        send_down(j).wait_recv()

    def upper(s, acc):
        for k in range(HALF):
            acc = finish(s * FACES + k, AB[partner[s, k]], acc)
        return acc

    acc1 = lax.fori_loop(0, SUBDOMS, upper, jnp.zeros((8, COLS), F32))

    @pl.loop(0, UP)
    def _(j):
        SU2[j] = TQ[INV[j]]
        send_up2(j).start()

    def lower(s, acc):
        for k in range(HALF):
            send_up(s * HALF + k).wait_recv()
            acc = finish(low(s, k), MT[s * HALF + k], acc)
        return acc

    acc1 = lax.fori_loop(0, SUBDOMS, lower, acc1)

    @pl.loop(UP, SLOTS)
    def _(j):
        send_down2(j).start()

    others = range(1, N_SUB)

    def over_sub(d):
        return send(RS.at[0], RS.at[d], z_s.at[d - 1], z_r.at[d - 1], along_sub(d))

    def work2(i, scalars=None):
        if i == 2:
            RS[0] = scalars
            for d in others:
                over_sub(d).start()

    sum_q = coarse_pass(1, Q, one_row(acc0), one_row(acc1), work2)
    for d in others:
        over_sub(d).wait_recv()
    sums = RS[0]
    for d in others:
        sums = sums + RS[d]
    norm0, curve0 = sums[0:1], sums[1:2]
    step0 = norm0 / curve0

    def resid(s, carry):
        n1, gq = carry
        for f in range(FACES):
            g = s * FACES + f
            q = Q[g]
            r = B[g] - step0 * q
            n1 = n1 + rows8(r * r)
            gq = gq + rows8(r * q)
            Q[g] = r
            RB[g] = r.astype(BF16)
        return n1, gq

    acc_n, acc_g = lax.fori_loop(
        0, SUBDOMS, resid, (jnp.zeros((8, COLS), F32), jnp.zeros((8, COLS), F32))
    )

    energy = jnp.zeros((8, COLS), F32)
    for s in range(SUBDOMS):
        field = RB[s * FACES : (s + 1) * FACES].reshape(ORDER, COLS)

        def tile(i, acc, s=s, field=field):
            part = mul(S[s, pl.ds(pl.multiple_of(i * TILE, TILE), TILE), :], field)
            for t in range(TILE // BLOCK):
                r = Q[s * FACES + i * (TILE // BLOCK) + t]
                acc = acc + rows8(r * part[t * BLOCK : (t + 1) * BLOCK])
            return acc

        energy = lax.fori_loop(0, ORDER // TILE, tile, energy)

    sum_r = sum_b - step0 * sum_q
    coarse_r = jnp.dot(K[...], sum_r, precision=EXACT, preferred_element_type=F32)
    energy = energy + rows8(sum_r * coarse_r) * (1.0 / N_GRP)

    def pair(first_jump, own, other, acc):
        second = own.astype(F32) - other.astype(F32)
        r = first_jump.astype(F32) - step0 * second
        return acc + rows8(r * r)

    def pair_low(j, acc):
        send_up2(j).wait_recv()
        g = low(j // HALF, j % HALF)
        return pair(JU[g], TQ[g], RU2[j], acc)

    energy = lax.fori_loop(0, UP, pair_low, energy)

    def pair_up(j, acc):
        send_down2(j).wait_recv()
        g = INV[j]
        return pair(JU[g], TQ[g], RD2[j - UP], acc)

    energy = lax.fori_loop(UP, SLOTS, pair_up, energy)

    AS[0, 0:1, :] = one_row(acc_n)
    AS[0, 1:2, :] = one_row(acc_g)
    AS[0, 2:3, :] = one_row(energy)
    AS[0, 3:8, :] = jnp.zeros((5, COLS), F32)

    def stage(i, buf, n, where):
        def copy(d):
            return send(AS.at[i], buf.at[d - 1], f_s.at[i, d - 1], f_r.at[i, d - 1], where(d))

        for d in range(1, n):
            copy(d).start()
        for d in range(1, n):
            copy(d).wait_recv()
        total = AS[i]
        for d in range(1, n):
            total = total + buf[d - 1]
        for d in range(1, n):
            copy(d).wait_send()
        return total

    AS[1] = stage(0, AX, SIDE, along_x)
    AS[2] = stage(1, AY, SIDE, along_y)
    sums = stage(2, AZ, N_SUB, along_sub)
    norm1, cross, energy1 = sums[0:1], sums[1:2], sums[2:3]
    beta = norm1 / norm0
    curve1 = energy1 + 2.0 * beta * cross + beta * beta * curve0
    step1 = norm1 / curve1
    with_load = step0 + step1 * beta

    def out_c(s):
        span = pl.ds(s * FACES, FACES)
        return pltpu.make_async_copy(Q.at[span], out_h.at[span], out_s.at[s])

    @pl.loop(0, SUBDOMS)
    def _(s):
        for f in range(FACES):
            g = s * FACES + f
            Q[g] = with_load * B[g] + step1 * Q[g]
        out_c(s).start()

    @pl.loop(0, SLOTS)
    def _(j):
        send_down(j).wait_send()
        send_up(j).wait_send()

    @pl.loop(0, UP)
    def _(j):
        send_up2(j).wait_send()

    @pl.loop(UP, SLOTS)
    def _(j):
        send_down2(j).wait_send()

    for d in others:
        over_sub(d).wait_send()
    for s in range(SUBDOMS):
        out_c(s).wait()


def on_device(schur, mortar, partner, corner_map, coarse_inv, load):
    vm, dma = pltpu.VMEM, pltpu.SemaphoreType.DMA
    anywhere = pl.BlockSpec(memory_space=pl.ANY)
    scalar = pl.BlockSpec(memory_space=pltpu.SMEM)
    faces_half = (ALL, BLOCK, COLS)
    slots_half = (SLOTS, BLOCK, COLS)
    scratch = [
        vm((SUBDOMS, ORDER, ORDER), BF16),
        vm((ALL, BLOCK, BLOCK), BF16),
        vm(faces_half, F32),
        vm((COARSE, COARSE), F32),
        vm(faces_half, BF16),
        vm(faces_half, F32),
        vm(faces_half, BF16),
        vm(faces_half, BF16),
        vm(slots_half, BF16),
        vm(slots_half, BF16),
        vm(slots_half, BF16),
        vm(faces_half, BF16),
        vm(faces_half, BF16),
        vm((UP, BLOCK, COLS), BF16),
        vm((UP, BLOCK, COLS), BF16),
        vm((SLOTS - UP, BLOCK, COLS), BF16),
        vm((ALL, COARSE), F32),
        vm((ALL, COLS), F32),
        vm((2, SIDE, 40, COLS), F32),
        vm((2, SIDE - 1, 40, COLS), F32),
        vm((2, SIDE, 16, COLS), F32),
        vm((2, SIDE - 1, 16, COLS), F32),
        vm((2, SIDE, 8, COLS), F32),
        vm((2, SIDE, 32, COLS), F32),
        vm((ALL, COLS), F32),
        vm((N_SUB, 8, COLS), F32),
        vm((3, 8, COLS), F32),
        vm((SIDE - 1, 8, COLS), F32),
        vm((SIDE - 1, 8, COLS), F32),
        vm((N_SUB - 1, 8, COLS), F32),
        pltpu.SMEM((SLOTS,), jnp.int32),
        dma((SUBDOMS,)), dma, dma((SUBDOMS,)), dma, dma((SUBDOMS,)),
        dma((SLOTS,)), dma((SLOTS,)), dma((SLOTS,)), dma((SLOTS,)),
        dma((SLOTS - UP,)), dma((SLOTS - UP,)), dma((UP,)), dma((UP,)),
        dma((2, 4, SIDE - 1)), dma((2, 4, SIDE - 1)),
        dma((N_SUB - 1,)), dma((N_SUB - 1,)),
        dma((3, N_SUB - 1)), dma((3, N_SUB - 1)),
    ]
    out = pl.pallas_call(
        kernel,
        out_shape=jax.ShapeDtypeStruct((ALL, BLOCK, COLS), F32),
        in_specs=[anywhere] * 4 + [scalar] * 2,
        out_specs=anywhere,
        scratch_shapes=scratch,
        compiler_params=pltpu.CompilerParams(
            collective_id=0, has_side_effects=True, vmem_limit_bytes=60 * 1024 * 1024
        ),
    )(
        schur,
        mortar.reshape(ALL, BLOCK, BLOCK),
        load.reshape(ALL, BLOCK, COLS),
        coarse_inv,
        partner,
        corner_map,
    )
    return out.reshape(SUBDOMS, ORDER, COLS)


def solution(mesh):
    return jax.shard_map(
        on_device,
        mesh=mesh,
        in_specs=(
            P(("sub", "grp"), None, None),
            P(("sub", "grp"), None, None, None),
            P(("sub", "grp"), None),
            P(("sub", "grp"), None),
            P("sub", None, None),
            P(("sub", "grp"), None, None),
        ),
        out_specs=P(("sub", "grp"), None, None),
        check_vma=False,
    )
```

time: 521 us -> 89.7 us (0.17)
  blocking collectives: 194 us -> 0 us
  waiting for transfers between devices: 161 us -> 0 us
  Pallas kernels: 0 us -> 83.6 us
  other arithmetic: 63.4 us -> 0 us
  local copies, waits for them, and re-layouts: 51.5 us -> 5.9 us
  matrix products: 32.3 us -> 0 us
  between operations: 13.6 us -> 0.01 us
    psum x3 -> x0, blocking collectives: 194 us -> none  [the longest x2 129 us: squares(): return lax.psum(jnp.sum(residual * residual, axis=(0, 1)), ('sub', 'grp'))]
    psum x2 -> x0, waiting for transfers between devices: 161 us -> none  [on_device(): lax.psum(local_sum.astype(jnp.bfloat16), 'grp').astype(jnp.float32)]
    pallas_call x0 -> x1, Pallas kernels: none -> 83.6 us  [on_device(): pl.pallas_call(kernel, out_shape=jax.ShapeDtypeStruct((ALL, BLOCK, COLS),...]
    dot_general x12 -> x0, matrix products: 32.3 us -> none  [the longest x2 19.3 us: face_terms(): jnp.einsum('sij,sjr->sir', schur, dir_half, preferred_element_type=jnp.fl...]
    reduce_sum x4 -> x0, other arithmetic: 26 us -> none  [the longest x2 14.9 us: on_device(): jnp.sum(direction * image, axis=(0, 1))]
    convert_element_type x5 -> x0, other arithmetic: 18.4 us -> none  [the longest x1 7.14 us: face_terms(): dir_half = direction.astype(jnp.bfloat16)]
    add x2 -> x0, local copies, waits for them, and re-layouts: 17.1 us -> none  [face_terms(): return stiff + pulled.reshape(subdoms, order, columns)]
    gather x4 -> x0, local copies, waits for them, and re-layouts: 10.5 us -> none  [the longest x2 6.65 us: face_terms(): upper_mate = jnp.take(above, mates, axis=0)]
  transfers between devices with their start and end apart: 6 -> 0, of which waited for: 2 -> 0; matrix products, arithmetic and copies ran while one was open for 5% -> 0% of each run, Pallas kernels for 0% -> 0%
where the time goes in v1:
time: 89.7 us; the launch traced here: 89.5 us
  Pallas kernels  83.6 us (93%)
  local copies, waits for them, and re-layouts  5.9 us (7%)
    pallas_call x1, Pallas kernels, on_device(): pl.pallas_call(kernel, out_shape=jax.ShapeDtypeStruct((ALL, BLOCK, COLS),...  83.6 us
    unnamed x1, local copies, waits for them, and re-layouts  5.9 us

profile of v1, /device:TPU:1, one launch (start us, length us, event | category | flops | bytes accessed | tf_op | source)
XLA Modules:
  0.0 89.5 jit_solution(5438255862933359097)
XLA Ops:
  0.0 83.6 %shard_map.64 = f32[32,128,384]{2,1,0:T(8,128)} custom-call(bf16[4,1024,1024]{2,1,0:T(8,128)(2,1)} %schur_h.1, bf16[32,128,128]{2,1,0:T(8,128)(2,1)} %bitcast.5, f32[32,128,384]{2,1,0:T(8,128)} %bitcast.4, f32[1,128,128]{2,1,0:T(8,128)} %coarse_h.1, s32[4,4]{1,0:T(4,128)} %partner.1, s32[4,8]{1,0:T(4,128)} %cmap.1), custom_call_target="tpu_custom_call" | custom-call | tf_op jit(solution)/shard_map/pallas_call | solution.py:449
  83.6 5.9 %copy.8 = f32[4,1024,384]{2,1,0:T(8,128)} copy(f32[4,1024,384]{2,1,0:T(8,128)} %bitcast.3) | data formatting | bytes 12582912

commit v2 on v0

v2 whole, which is shorter than its diff:
```python
import functools

import jax
import jax.numpy as jnp
from jax import lax
from jax.experimental import pallas as pl
from jax.experimental.pallas import tpu as pltpu
from jax.sharding import PartitionSpec as P

F32, BF16 = jnp.float32, jnp.bfloat16
SUBDOMS, HALF, FACES = 4, 4, 8
BLOCK, COLS, ORDER = 128, 384, 1024
ALL, SLOTS, COARSE = 32, 16, 128
OWN = COARSE // 16
N_SUB = 8
N_GRP = 16
UP = 8
TILE = 512
PER = TILE // BLOCK
MESH = pl.DeviceIdType.MESH
EXACT = lax.Precision.HIGHEST


def low(s, k):
    return s * FACES + HALF + k


def rows8(a):
    return jnp.sum(a.reshape(BLOCK // 8, 8, COLS), axis=0)


def one_row(acc):
    return jnp.sum(acc, axis=0, keepdims=True)


def mul(a, b):
    return jnp.dot(a, b, preferred_element_type=F32)


def mul_t(a, b):
    return lax.dot_general(a, b, (((0,), (0,)), ((), ())), preferred_element_type=F32)


def kernel(
    schur_h, mortar_h, load_h, coarse_h, partner, cmap, out,
    S, M, B, K, VB, Q, RB, TR, SU, AB, MT, TQ, SU2, RU2, RD2,
    OH, CR, CA, CX, RX, GX, AS, AG, AZ, INV,
    load_s, mort_s, schur_s, coarse_s,
    sd_s, sd_r, su_s, su_r, td_s, td_r, tu_s, tu_r,
    g_s, g_r, z_s, z_r,
):
    sub, grp = lax.axis_index("sub"), lax.axis_index("grp")
    above, below = (sub + 1) % N_SUB, (sub + N_SUB - 1) % N_SUB

    def in_group(d):
        return {"grp": (grp + d) % N_GRP}

    def over_sub(d):
        return {"sub": (sub + d) % N_SUB}

    def send(src, dst, ssem, rsem, device):
        return pltpu.make_async_remote_copy(
            src_ref=src, dst_ref=dst, send_sem=ssem, recv_sem=rsem,
            device_id=device, device_id_type=MESH,
        )

    def send_down(j):
        g = low(j // HALF, j % HALF)
        return send(TR.at[g], AB.at[j], sd_s.at[j], sd_r.at[j], {"sub": below})

    def send_up(j):
        return send(SU.at[j], MT.at[j], su_s.at[j], su_r.at[j], {"sub": above})

    def send_up2(j):
        return send(SU2.at[j], RU2.at[j], tu_s.at[j], tu_r.at[j], {"sub": above})

    def send_down2(j):
        g, i = low(j // HALF, j % HALF), j - UP
        return send(TQ.at[g], RD2.at[i], td_s.at[i], td_r.at[i], {"sub": below})

    def scatter_rows(p, d):
        to = (grp + d) % N_GRP
        return send(
            CX.at[p, to], RX.at[p, d - 1], g_s.at[p, 0, d - 1], g_r.at[p, 0, d - 1], in_group(d)
        )

    def gather_rows(p, d):
        return send(
            GX.at[p, grp], GX.at[p, grp], g_s.at[p, 1, d - 1], g_r.at[p, 1, d - 1], in_group(d)
        )

    def sum_grp(p, d):
        return send(
            AS.at[p, 0], AG.at[p, d - 1], g_s.at[p, 2, d - 1], g_r.at[p, 2, d - 1], in_group(d)
        )

    def sum_sub(p, d):
        return send(AS.at[p, 1], AZ.at[p, d - 1], z_s.at[p, d - 1], z_r.at[p, d - 1], over_sub(d))

    def start_all(copy, p, n):
        @pl.loop(1, n)
        def _(d):
            copy(p, d).start()

    def take_all(copy, p, n):
        @pl.loop(1, n)
        def _(d):
            copy(p, d).wait_recv()

    def end_all(copy, p, n):
        @pl.loop(1, n)
        def _(d):
            copy(p, d).wait_send()

    mort_c = pltpu.make_async_copy(mortar_h, M, mort_s)

    def load_c(s):
        span = pl.ds(s * FACES, FACES)
        return pltpu.make_async_copy(load_h.at[span], B.at[span], load_s.at[s])

    def schur_c(s):
        return pltpu.make_async_copy(schur_h.at[s], S.at[s], schur_s.at[s])

    coarse_c = pltpu.make_async_copy(coarse_h.at[0], K, coarse_s)
    for s in range(SUBDOMS):
        load_c(s).start()
    mort_c.start()
    coarse_c.start()
    for s in range(SUBDOMS):
        schur_c(s).start()

    barrier = pltpu.get_barrier_semaphore()

    @pl.loop(1, N_GRP)
    def _(d):
        pl.semaphore_signal(barrier, inc=1, device_id=in_group(d), device_id_type=MESH)

    @pl.loop(1, N_SUB)
    def _(d):
        pl.semaphore_signal(barrier, inc=1, device_id=over_sub(d), device_id_type=MESH)

    @pl.loop(0, SLOTS)
    def _(j):
        found = jnp.int32(0)
        for u in range(SLOTS):
            at = (u // HALF) * FACES + u % HALF
            found = jnp.where(partner[u // HALF, u % HALF] == j, at, found)
        INV[j] = found

    lanes = lax.broadcasted_iota(jnp.int32, (1, COARSE), 1)

    @pl.loop(0, SUBDOMS)
    def _(s):
        for c in range(FACES):
            OH[pl.ds(s * FACES + c, 1), :] = jnp.where(lanes == cmap[s, c], 1.0, 0.0).astype(F32)

    def coarse_start(p):
        local = lax.dot_general(
            OH[...], CR[...], (((0,), (0,)), ((), ())), precision=EXACT, preferred_element_type=F32
        )
        CX[p] = local.reshape(N_GRP, OWN, COLS)
        start_all(scatter_rows, p, N_GRP)

    def coarse_middle(p):
        take_all(scatter_rows, p, N_GRP)
        total = CX[p, grp]
        for d in range(1, N_GRP):
            total = total + RX[p, d - 1]
        GX[p, grp] = total
        start_all(gather_rows, p, N_GRP)

    def coarse_end(p):
        take_all(gather_rows, p, N_GRP)
        vector = GX[p].reshape(COARSE, COLS)
        value = jnp.dot(K[...], vector, precision=EXACT, preferred_element_type=F32)
        return value, one_row(jnp.sum((vector * value).reshape(N_GRP, 8, COLS), axis=0))

    for s in range(SUBDOMS):
        load_c(s).wait()

    @pl.loop(0, SUBDOMS)
    def _(s):
        for f in range(FACES):
            g = s * FACES + f
            CR[pl.ds(g, 1), :] = B[g, 0:1, :]

    pl.semaphore_wait(barrier, N_GRP + N_SUB - 2)
    coarse_start(0)
    mort_c.wait()

    def first_low(i, acc):
        s = SUBDOMS - 1 - i
        for k in reversed(range(HALF)):
            j, g = s * HALF + k, low(s, k)
            b = B[g]
            acc = acc + rows8(b * b)
            half = b.astype(BF16)
            VB[g] = half
            TR[g] = mul(M[g], half).astype(BF16)
            send_down(j).start()
        return acc

    def first_up(s, acc):
        for k in range(HALF):
            g = s * FACES + k
            b = B[g]
            acc = acc + rows8(b * b)
            half = b.astype(BF16)
            VB[g] = half
            TR[g] = mul(M[g], half).astype(BF16)
        return acc

    zero8 = jnp.zeros((8, COLS), F32)
    acc0 = lax.fori_loop(0, SUBDOMS, first_up, zero8)

    @pl.loop(0, SLOTS)
    def _(j):
        SU[j] = TR[INV[j]]
        send_up(j).start()

    acc0 = lax.fori_loop(0, SUBDOMS, first_low, acc0)

    def stiff(s, acc):
        schur_c(s).wait()
        field = VB[s * FACES : (s + 1) * FACES].reshape(ORDER, COLS)

        def tile(i, acc):
            part = mul(S[s, pl.ds(pl.multiple_of(i * TILE, TILE), TILE), :], field)
            for t in range(PER):
                g = s * FACES + i * PER + t
                q = part[t * BLOCK : (t + 1) * BLOCK]
                Q[g] = q
                acc = acc + rows8(B[g] * q)
            return acc

        return lax.fori_loop(0, ORDER // TILE, tile, acc)

    acc1 = stiff(0, zero8)
    acc1 = stiff(1, acc1)
    coarse_c.wait()
    coarse_middle(0)
    acc1 = stiff(2, acc1)
    acc1 = stiff(3, acc1)

    def jump2(own, mate):
        d = (own.astype(F32) - mate.astype(F32)).astype(BF16).astype(F32)
        return rows8(d * d)

    def count_low(j, acc):
        send_up(j).wait_recv()
        return acc + jump2(TR[low(j // HALF, j % HALF)], MT[j])

    def count_up(i, acc):
        j = SLOTS - 1 - i
        send_down(j).wait_recv()
        return acc + jump2(TR[INV[j]], AB[j])

    acc1 = lax.fori_loop(0, UP, count_low, acc1)
    acc1 = lax.fori_loop(0, SLOTS - UP, count_up, acc1)

    def sum_start(p, values):
        for i, v in enumerate(values):
            AS[p, 0, i : i + 1, :] = one_row(v)
        AS[p, 0, len(values) : 8, :] = jnp.zeros((8 - len(values), COLS), F32)
        start_all(sum_grp, p, N_GRP)

    def sum_middle(p, row, extra):
        take_all(sum_grp, p, N_GRP)
        total = AS[p, 0]
        for d in range(1, N_GRP):
            total = total + AG[p, d - 1]
        AS[p, 1] = total
        AS[p, 1, row : row + 1, :] = AS[p, 1, row : row + 1, :] + extra
        start_all(sum_sub, p, N_SUB)

    def sum_end(p):
        take_all(sum_sub, p, N_SUB)
        total = AS[p, 1]
        for d in range(1, N_SUB):
            total = total + AZ[p, d - 1]
        return total

    sum_start(0, [acc0, acc1])
    coarse_val, coarse_energy = coarse_end(0)
    CA[...] = jnp.dot(OH[...], coarse_val, precision=EXACT, preferred_element_type=F32)

    @pl.loop(0, SUBDOMS)
    def _(s):
        for f in range(FACES):
            g = s * FACES + f
            Q[g, 0:1, :] = Q[g, 0:1, :] + CA[pl.ds(g, 1), :]

    def finish(g, mate):
        jump = (TR[g].astype(F32) - mate.astype(F32)).astype(BF16)
        Q[g] = Q[g] + mul_t(M[g], jump)

    def lower(s, wait):
        for k in range(HALF):
            if wait:
                send_up(s * HALF + k).wait_recv()
            finish(low(s, k), MT[s * HALF + k])

    @pl.loop(0, UP // HALF)
    def _(s):
        lower(s, False)

    sum_middle(0, 1, coarse_energy)

    @pl.loop(UP // HALF, SUBDOMS)
    def _(s):
        lower(s, True)

    @pl.loop(0, UP)
    def _(j):
        send_down(j).wait_recv()

    @pl.loop(0, SUBDOMS)
    def _(s):
        for k in range(HALF):
            finish(s * FACES + k, AB[partner[s, k]])

    sums = sum_end(0)
    norm0, curve0 = sums[0:1], sums[1:2]
    step0 = norm0 / curve0

    @pl.loop(0, SUBDOMS)
    def _(s):
        for f in range(FACES):
            g = s * FACES + f
            CR[pl.ds(g, 1), :] = B[g, 0:1, :] - step0 * Q[g, 0:1, :]

    coarse_start(1)

    def resid(g, carry):
        n1, gq = carry
        q = Q[g]
        r = B[g] - step0 * q
        half = r.astype(BF16)
        Q[g] = r
        RB[g] = half
        TQ[g] = mul(M[g], half).astype(BF16)
        return n1 + rows8(r * r), gq + rows8(r * q)

    def resid_up(s, carry):
        for k in range(HALF):
            carry = resid(s * FACES + k, carry)
        return carry

    def resid_low(s, carry):
        for k in range(HALF):
            carry = resid(low(s, k), carry)
        return carry

    def resid_low_send(s, carry):
        for k in range(HALF):
            carry = resid(low(s, k), carry)
            send_down2(s * HALF + k).start()
        return carry

    carry = lax.fori_loop(UP // HALF, SUBDOMS, resid_low_send, (zero8, zero8))
    carry = lax.fori_loop(0, SUBDOMS, resid_up, carry)

    @pl.loop(0, UP)
    def _(j):
        SU2[j] = TQ[INV[j]]
        send_up2(j).start()

    acc_n, acc_g = lax.fori_loop(0, UP // HALF, resid_low, carry)

    def inner(s, acc):
        field = RB[s * FACES : (s + 1) * FACES].reshape(ORDER, COLS)

        def tile(i, acc):
            part = mul(S[s, pl.ds(pl.multiple_of(i * TILE, TILE), TILE), :], field)
            for t in range(PER):
                acc = acc + rows8(Q[s * FACES + i * PER + t] * part[t * BLOCK : (t + 1) * BLOCK])
            return acc

        return lax.fori_loop(0, ORDER // TILE, tile, acc)

    energy = inner(0, zero8)
    energy = inner(1, energy)
    energy = inner(2, energy)
    coarse_middle(1)
    energy = inner(3, energy)

    def pair2(own, mate):
        d = own.astype(F32) - mate.astype(F32)
        return rows8(d * d)

    def pair_low(j, acc):
        send_up2(j).wait_recv()
        return acc + pair2(TQ[low(j // HALF, j % HALF)], RU2[j])

    def pair_up(j, acc):
        send_down2(j).wait_recv()
        return acc + pair2(TQ[INV[j]], RD2[j - UP])

    energy = lax.fori_loop(UP, SLOTS, pair_up, energy)
    energy = lax.fori_loop(0, UP, pair_low, energy)

    sum_start(1, [acc_n, acc_g, energy])
    _, coarse_energy = coarse_end(1)
    sum_middle(1, 2, coarse_energy)

    @pl.loop(0, SLOTS)
    def _(j):
        send_down(j).wait_send()
        send_up(j).wait_send()

    @pl.loop(0, UP)
    def _(j):
        send_up2(j).wait_send()

    @pl.loop(UP, SLOTS)
    def _(j):
        send_down2(j).wait_send()

    for p in range(2):
        end_all(scatter_rows, p, N_GRP)
        end_all(gather_rows, p, N_GRP)
        end_all(sum_grp, p, N_GRP)
    end_all(sum_sub, 0, N_SUB)

    sums = sum_end(1)
    norm1, cross, energy1 = sums[0:1], sums[1:2], sums[2:3]
    beta = norm1 / norm0
    curve1 = energy1 + 2.0 * beta * cross + beta * beta * curve0
    step1 = norm1 / curve1
    with_load = step0 + step1 * beta

    @pl.loop(0, SUBDOMS)
    def _(s):
        for f in range(FACES):
            g = s * FACES + f
            out[g] = with_load * B[g] + step1 * Q[g]

    end_all(sum_sub, 1, N_SUB)


def on_device(schur, mortar, partner, corner_map, coarse_inv, load):
    vm, dma = pltpu.VMEM, pltpu.SemaphoreType.DMA
    anywhere = pl.BlockSpec(memory_space=pl.ANY)
    scalar = pl.BlockSpec(memory_space=pltpu.SMEM)
    faces_half = (ALL, BLOCK, COLS)
    slots_half = (SLOTS, BLOCK, COLS)
    scratch = [
        vm((SUBDOMS, ORDER, ORDER), BF16),
        vm((ALL, BLOCK, BLOCK), BF16),
        vm(faces_half, F32),
        vm((COARSE, COARSE), F32),
        vm(faces_half, BF16),
        vm(faces_half, F32),
        vm(faces_half, BF16),
        vm(faces_half, BF16),
        vm(slots_half, BF16),
        vm(slots_half, BF16),
        vm(slots_half, BF16),
        vm(faces_half, BF16),
        vm((UP, BLOCK, COLS), BF16),
        vm((UP, BLOCK, COLS), BF16),
        vm((SLOTS - UP, BLOCK, COLS), BF16),
        vm((ALL, COARSE), F32),
        vm((ALL, COLS), F32),
        vm((ALL, COLS), F32),
        vm((2, N_GRP, OWN, COLS), F32),
        vm((2, N_GRP - 1, OWN, COLS), F32),
        vm((2, N_GRP, OWN, COLS), F32),
        vm((2, 2, 8, COLS), F32),
        vm((2, N_GRP - 1, 8, COLS), F32),
        vm((2, N_SUB - 1, 8, COLS), F32),
        pltpu.SMEM((SLOTS,), jnp.int32),
        dma((SUBDOMS,)), dma, dma((SUBDOMS,)), dma,
        dma((SLOTS,)), dma((SLOTS,)), dma((SLOTS,)), dma((SLOTS,)),
        dma((SLOTS - UP,)), dma((SLOTS - UP,)), dma((UP,)), dma((UP,)),
        dma((2, 3, N_GRP - 1)), dma((2, 3, N_GRP - 1)),
        dma((2, N_SUB - 1)), dma((2, N_SUB - 1)),
    ]
    out = pl.pallas_call(
        kernel,
        out_shape=pltpu.VMEM(faces_half, F32),
        in_specs=[anywhere] * 4 + [scalar] * 2,
        out_specs=pl.BlockSpec(memory_space=pltpu.VMEM),
        scratch_shapes=scratch,
        compiler_params=pltpu.CompilerParams(
            collective_id=0, has_side_effects=True, vmem_limit_bytes=50 * 1024 * 1024
        ),
    )(
        schur,
        mortar.reshape(ALL, BLOCK, BLOCK),
        load.reshape(ALL, BLOCK, COLS),
        coarse_inv,
        partner,
        corner_map,
    )
    return out.reshape(SUBDOMS, ORDER, COLS)


def solution(mesh):
    return jax.shard_map(
        on_device,
        mesh=mesh,
        in_specs=(
            P(("sub", "grp"), None, None),
            P(("sub", "grp"), None, None, None),
            P(("sub", "grp"), None),
            P(("sub", "grp"), None),
            P("sub", None, None),
            P(("sub", "grp"), None, None),
        ),
        out_specs=P(("sub", "grp"), None, None),
        check_vma=False,
    )
```

time: 521 us -> 64.1 us (0.12)
  blocking collectives: 194 us -> 0 us
  waiting for transfers between devices: 161 us -> 0 us
  other arithmetic: 63.4 us -> 0 us
  Pallas kernels: 0 us -> 61.2 us
  local copies, waits for them, and re-layouts: 51.5 us -> 2.71 us
  matrix products: 32.3 us -> 0 us
  between operations: 13.6 us -> 0.01 us
    psum x3 -> x0, blocking collectives: 194 us -> none  [the longest x2 129 us: squares(): return lax.psum(jnp.sum(residual * residual, axis=(0, 1)), ('sub', 'grp'))]
    psum x2 -> x0, waiting for transfers between devices: 161 us -> none  [on_device(): lax.psum(local_sum.astype(jnp.bfloat16), 'grp').astype(jnp.float32)]
    pallas_call x0 -> x1, Pallas kernels: none -> 61.2 us  [on_device(): pl.pallas_call(kernel, out_shape=pltpu.VMEM(faces_half, F32), in_specs=[a...]
    dot_general x12 -> x0, matrix products: 32.3 us -> none  [the longest x2 19.3 us: face_terms(): jnp.einsum('sij,sjr->sir', schur, dir_half, preferred_element_type=jnp.fl...]
    reduce_sum x4 -> x0, other arithmetic: 26 us -> none  [the longest x2 14.9 us: on_device(): jnp.sum(direction * image, axis=(0, 1))]
    convert_element_type x5 -> x0, other arithmetic: 18.4 us -> none  [the longest x1 7.14 us: face_terms(): dir_half = direction.astype(jnp.bfloat16)]
    add x2 -> x0, local copies, waits for them, and re-layouts: 17.1 us -> none  [face_terms(): return stiff + pulled.reshape(subdoms, order, columns)]
    gather x4 -> x0, local copies, waits for them, and re-layouts: 10.5 us -> none  [the longest x2 6.65 us: face_terms(): upper_mate = jnp.take(above, mates, axis=0)]
  transfers between devices with their start and end apart: 6 -> 0, of which waited for: 2 -> 0; matrix products, arithmetic and copies ran while one was open for 5% -> 0% of each run, Pallas kernels for 0% -> 0%
where the time goes in v2:
time: 64.1 us; the launch traced here: 63.9 us
  Pallas kernels  61.2 us (95%)
  local copies, waits for them, and re-layouts  2.71 us (4%)
    pallas_call x1, Pallas kernels, on_device(): pl.pallas_call(kernel, out_shape=pltpu.VMEM(faces_half, F32), in_specs=[a...  61.2 us
    unnamed x1, local copies, waits for them, and re-layouts  2.71 us

profile of v2, /device:TPU:1, one launch (start us, length us, event | category | flops | bytes accessed | tf_op | source)
XLA Modules:
  0.0 63.9 jit_solution(3872678570455102346)
XLA Ops:
  0.0 61.2 %shard_map.64 = f32[32,128,384]{2,1,0:T(8,128)S(1)} custom-call(bf16[4,1024,1024]{2,1,0:T(8,128)(2,1)} %schur_h.1, bf16[32,128,128]{2,1,0:T(8,128)(2,1)} %bitcast.5, f32[32,128,384]{2,1,0:T(8,128)} %bitcast.4, f32[1,128,128]{2,1,0:T(8,128)} %coarse_h.1, s32[4,4]{1,0:T(4,128)} %partner.1, s32[4,8]{1,0:T(4,128)} %cmap.1), custom_call_target="tpu_custom_call" | custom-call | tf_op jit(solution)/shard_map/pallas_call | solution.py:479
  61.2 2.7 %copy.8 = f32[4,1024,384]{2,1,0:T(8,128)} copy(f32[4,1024,384]{2,1,0:T(8,128)S(1)} %bitcast.3) | data formatting | bytes 12582912

commit v3 on v2

--- a/solution.py
+++ b/solution.py
@@ -15,7 +15,7 @@
 N_SUB = 8
 N_GRP = 16
 UP = 8
-TILE = 512
+TILE = 1024
 PER = TILE // BLOCK
 MESH = pl.DeviceIdType.MESH
 EXACT = lax.Precision.HIGHEST
@@ -42,8 +42,8 @@
 
 
 def kernel(
-    schur_h, mortar_h, load_h, coarse_h, partner, cmap, out,
-    S, M, B, K, VB, Q, RB, TR, SU, AB, MT, TQ, SU2, RU2, RD2,
+    schur_h, mortar_h, load_h, coarse_h, partner, cmap, B, Q, COEF,
+    S, M, K, VB, RB, TR, SU, AB, MT, PP, TQ, TU, SU2, RU2, RD2,
     OH, CR, CA, CX, RX, GX, AS, AG, AZ, INV,
     load_s, mort_s, schur_s, coarse_s,
     sd_s, sd_r, su_s, su_r, td_s, td_r, tu_s, tu_r,
@@ -112,6 +112,16 @@
         def _(d):
             copy(p, d).wait_send()
 
+    barrier = pltpu.get_barrier_semaphore()
+
+    @pl.loop(1, N_GRP)
+    def _(d):
+        pl.semaphore_signal(barrier, inc=1, device_id=in_group(d), device_id_type=MESH)
+
+    @pl.loop(1, N_SUB)
+    def _(d):
+        pl.semaphore_signal(barrier, inc=1, device_id=over_sub(d), device_id_type=MESH)
+
     mort_c = pltpu.make_async_copy(mortar_h, M, mort_s)
 
     def load_c(s):
@@ -122,22 +132,10 @@
         return pltpu.make_async_copy(schur_h.at[s], S.at[s], schur_s.at[s])
 
     coarse_c = pltpu.make_async_copy(coarse_h.at[0], K, coarse_s)
+    mort_c.start()
     for s in range(SUBDOMS):
         load_c(s).start()
-    mort_c.start()
     coarse_c.start()
-    for s in range(SUBDOMS):
-        schur_c(s).start()
-
-    barrier = pltpu.get_barrier_semaphore()
-
-    @pl.loop(1, N_GRP)
-    def _(d):
-        pl.semaphore_signal(barrier, inc=1, device_id=in_group(d), device_id_type=MESH)
-
-    @pl.loop(1, N_SUB)
-    def _(d):
-        pl.semaphore_signal(barrier, inc=1, device_id=over_sub(d), device_id_type=MESH)
 
     @pl.loop(0, SLOTS)
     def _(j):
@@ -169,14 +167,45 @@
         GX[p, grp] = total
         start_all(gather_rows, p, N_GRP)
 
-    def coarse_end(p):
+    def coarse_end(p, step):
         take_all(gather_rows, p, N_GRP)
-        vector = GX[p].reshape(COARSE, COLS)
+        vector = GX[0].reshape(COARSE, COLS)
+        if p == 1:
+            vector = vector - step * GX[1].reshape(COARSE, COLS)
         value = jnp.dot(K[...], vector, precision=EXACT, preferred_element_type=F32)
         return value, one_row(jnp.sum((vector * value).reshape(N_GRP, 8, COLS), axis=0))
 
+    def first(g, acc):
+        b = B[g]
+        half = b.astype(BF16)
+        VB[g] = half
+        TR[g] = mul(M[g], half).astype(BF16)
+        return acc + rows8(b * b)
+
+    def first_up(s, acc):
+        load_c(s).wait()
+        for k in range(HALF):
+            acc = first(s * FACES + k, acc)
+        return acc
+
+    zero8 = jnp.zeros((8, COLS), F32)
+    mort_c.wait()
+    acc0 = lax.fori_loop(0, SUBDOMS, first_up, zero8)
     for s in range(SUBDOMS):
-        load_c(s).wait()
+        schur_c(s).start()
+    pl.semaphore_wait(barrier, N_GRP + N_SUB - 2)
+
+    def first_low(i, acc):
+        for k in range(HALF):
+            up = i * HALF + k
+            SU[up] = TR[INV[up]]
+            send_up(up).start()
+            s, t = SUBDOMS - 1 - i, HALF - 1 - k
+            acc = first(low(s, t), acc)
+            send_down(s * HALF + t).start()
+        return acc
+
+    acc0 = lax.fori_loop(0, SUBDOMS, first_low, acc0)
 
     @pl.loop(0, SUBDOMS)
     def _(s):
@@ -184,41 +213,7 @@
             g = s * FACES + f
             CR[pl.ds(g, 1), :] = B[g, 0:1, :]
 
-    pl.semaphore_wait(barrier, N_GRP + N_SUB - 2)
     coarse_start(0)
-    mort_c.wait()
-
-    def first_low(i, acc):
-        s = SUBDOMS - 1 - i
-        for k in reversed(range(HALF)):
-            j, g = s * HALF + k, low(s, k)
-            b = B[g]
-            acc = acc + rows8(b * b)
-            half = b.astype(BF16)
-            VB[g] = half
-            TR[g] = mul(M[g], half).astype(BF16)
-            send_down(j).start()
-        return acc
-
-    def first_up(s, acc):
-        for k in range(HALF):
-            g = s * FACES + k
-            b = B[g]
-            acc = acc + rows8(b * b)
-            half = b.astype(BF16)
-            VB[g] = half
-            TR[g] = mul(M[g], half).astype(BF16)
-        return acc
-
-    zero8 = jnp.zeros((8, COLS), F32)
-    acc0 = lax.fori_loop(0, SUBDOMS, first_up, zero8)
-
-    @pl.loop(0, SLOTS)
-    def _(j):
-        SU[j] = TR[INV[j]]
-        send_up(j).start()
-
-    acc0 = lax.fori_loop(0, SUBDOMS, first_low, acc0)
 
     def stiff(s, acc):
         schur_c(s).wait()
@@ -237,26 +232,35 @@
 
     acc1 = stiff(0, zero8)
     acc1 = stiff(1, acc1)
+    acc1 = stiff(2, acc1)
+    acc1 = stiff(3, acc1)
     coarse_c.wait()
     coarse_middle(0)
-    acc1 = stiff(2, acc1)
-    acc1 = stiff(3, acc1)
-
-    def jump2(own, mate):
-        d = (own.astype(F32) - mate.astype(F32)).astype(BF16).astype(F32)
+
+    def jump_of(own, mate):
+        return (own.astype(F32) - mate.astype(F32)).astype(BF16)
+
+    def square(jump):
+        d = jump.astype(F32)
         return rows8(d * d)
 
-    def count_low(j, acc):
-        send_up(j).wait_recv()
-        return acc + jump2(TR[low(j // HALF, j % HALF)], MT[j])
-
-    def count_up(i, acc):
+    def pull(i):
+        send_up(i).wait_recv()
+        g = low(i // HALF, i % HALF)
+        jump_l = jump_of(TR[g], MT[i])
+        Q[g] = Q[g] + mul_t(M[g], jump_l)
         j = SLOTS - 1 - i
         send_down(j).wait_recv()
-        return acc + jump2(TR[INV[j]], AB[j])
-
-    acc1 = lax.fori_loop(0, UP, count_low, acc1)
-    acc1 = lax.fori_loop(0, SLOTS - UP, count_up, acc1)
+        g = INV[j]
+        jump_u = jump_of(TR[g], AB[j])
+        PP[j] = mul_t(M[g], jump_u)
+        return jump_l, jump_u
+
+    def pull_count(i, acc):
+        jump_l, jump_u = pull(i)
+        return acc + square(jump_l) + square(jump_u)
+
+    acc1 = lax.fori_loop(0, UP, pull_count, acc1)
 
     def sum_start(p, values):
         for i, v in enumerate(values):
@@ -281,7 +285,7 @@
         return total
 
     sum_start(0, [acc0, acc1])
-    coarse_val, coarse_energy = coarse_end(0)
+    coarse_val, coarse_energy = coarse_end(0, None)
     CA[...] = jnp.dot(OH[...], coarse_val, precision=EXACT, preferred_element_type=F32)
 
     @pl.loop(0, SUBDOMS)
@@ -290,82 +294,64 @@
             g = s * FACES + f
             Q[g, 0:1, :] = Q[g, 0:1, :] + CA[pl.ds(g, 1), :]
 
-    def finish(g, mate):
-        jump = (TR[g].astype(F32) - mate.astype(F32)).astype(BF16)
-        Q[g] = Q[g] + mul_t(M[g], jump)
-
-    def lower(s, wait):
-        for k in range(HALF):
-            if wait:
-                send_up(s * HALF + k).wait_recv()
-            finish(low(s, k), MT[s * HALF + k])
-
-    @pl.loop(0, UP // HALF)
-    def _(s):
-        lower(s, False)
+    @pl.loop(UP, 12)
+    def _(i):
+        pull(i)
 
     sum_middle(0, 1, coarse_energy)
 
-    @pl.loop(UP // HALF, SUBDOMS)
-    def _(s):
-        lower(s, True)
-
-    @pl.loop(0, UP)
-    def _(j):
-        send_down(j).wait_recv()
-
-    @pl.loop(0, SUBDOMS)
-    def _(s):
-        for k in range(HALF):
-            finish(s * FACES + k, AB[partner[s, k]])
-
-    sums = sum_end(0)
-    norm0, curve0 = sums[0:1], sums[1:2]
-    step0 = norm0 / curve0
+    @pl.loop(12, SLOTS)
+    def _(i):
+        pull(i)
+
+    def image_send(i, none):
+        j = UP + i
+        g = low(j // HALF, j % HALF)
+        TQ[g] = mul(M[g], Q[g].astype(BF16)).astype(BF16)
+        send_down2(j).start()
+        g = INV[i]
+        SU2[i] = mul(M[g], (Q[g] + PP[i]).astype(BF16)).astype(BF16)
+        send_up2(i).start()
+        return none
+
+    lax.fori_loop(0, UP, image_send, 0)
 
     @pl.loop(0, SUBDOMS)
     def _(s):
         for f in range(FACES):
             g = s * FACES + f
-            CR[pl.ds(g, 1), :] = B[g, 0:1, :] - step0 * Q[g, 0:1, :]
+            row = Q[g, 0:1, :]
+            if f < HALF:
+                row = row + PP[partner[s, f], 0:1, :]
+            CR[pl.ds(g, 1), :] = row
 
     coarse_start(1)
 
-    def resid(g, carry):
+    @pl.loop(0, UP)
+    def _(i):
+        g = low(i // HALF, i % HALF)
+        TQ[g] = mul(M[g], Q[g].astype(BF16)).astype(BF16)
+        g = INV[UP + i]
+        TU[i] = mul(M[g], (Q[g] + PP[UP + i]).astype(BF16)).astype(BF16)
+
+    sums = sum_end(0)
+    norm0, curve0 = sums[0:1], sums[1:2]
+    step0 = norm0 / curve0
+
+    def resid(s, carry):
         n1, gq = carry
-        q = Q[g]
-        r = B[g] - step0 * q
-        half = r.astype(BF16)
-        Q[g] = r
-        RB[g] = half
-        TQ[g] = mul(M[g], half).astype(BF16)
-        return n1 + rows8(r * r), gq + rows8(r * q)
-
-    def resid_up(s, carry):
-        for k in range(HALF):
-            carry = resid(s * FACES + k, carry)
-        return carry
-
-    def resid_low(s, carry):
-        for k in range(HALF):
-            carry = resid(low(s, k), carry)
-        return carry
-
-    def resid_low_send(s, carry):
-        for k in range(HALF):
-            carry = resid(low(s, k), carry)
-            send_down2(s * HALF + k).start()
-        return carry
-
-    carry = lax.fori_loop(UP // HALF, SUBDOMS, resid_low_send, (zero8, zero8))
-    carry = lax.fori_loop(0, SUBDOMS, resid_up, carry)
-
-    @pl.loop(0, UP)
-    def _(j):
-        SU2[j] = TQ[INV[j]]
-        send_up2(j).start()
-
-    acc_n, acc_g = lax.fori_loop(0, UP // HALF, resid_low, carry)
+        for f in range(FACES):
+            g = s * FACES + f
+            q = Q[g]
+            if f < HALF:
+                q = q + PP[partner[s, f]]
+            r = B[g] - step0 * q
+            Q[g] = r
+            RB[g] = r.astype(BF16)
+            n1, gq = n1 + rows8(r * r), gq + rows8(r * q)
+        return n1, gq
+
+    acc_n, acc_g = lax.fori_loop(0, SUBDOMS, resid, (zero8, zero8))
 
     def inner(s, acc):
         field = RB[s * FACES : (s + 1) * FACES].reshape(ORDER, COLS)
@@ -380,27 +366,29 @@
 
     energy = inner(0, zero8)
     energy = inner(1, energy)
+    coarse_middle(1)
     energy = inner(2, energy)
-    coarse_middle(1)
     energy = inner(3, energy)
 
-    def pair2(own, mate):
-        d = own.astype(F32) - mate.astype(F32)
+    def pair2(first_jump, own, mate):
+        d = first_jump.astype(F32) - step0 * (own.astype(F32) - mate.astype(F32))
         return rows8(d * d)
 
     def pair_low(j, acc):
         send_up2(j).wait_recv()
-        return acc + pair2(TQ[low(j // HALF, j % HALF)], RU2[j])
+        g = low(j // HALF, j % HALF)
+        return acc + pair2(jump_of(TR[g], MT[j]), TQ[g], RU2[j])
 
     def pair_up(j, acc):
         send_down2(j).wait_recv()
-        return acc + pair2(TQ[INV[j]], RD2[j - UP])
+        g = INV[j]
+        return acc + pair2(jump_of(TR[g], AB[j]), TU[j - UP], RD2[j - UP])
 
     energy = lax.fori_loop(UP, SLOTS, pair_up, energy)
     energy = lax.fori_loop(0, UP, pair_low, energy)
 
     sum_start(1, [acc_n, acc_g, energy])
-    _, coarse_energy = coarse_end(1)
+    _, coarse_energy = coarse_end(1, step0)
     sum_middle(1, 2, coarse_energy)
 
     @pl.loop(0, SLOTS)
@@ -429,12 +417,9 @@
     step1 = norm1 / curve1
     with_load = step0 + step1 * beta
 
-    @pl.loop(0, SUBDOMS)
-    def _(s):
-        for f in range(FACES):
-            g = s * FACES + f
-            out[g] = with_load * B[g] + step1 * Q[g]
-
+    COEF[0:1, :] = with_load
+    COEF[1:2, :] = step1
+    COEF[2:8, :] = jnp.zeros((6, COLS), F32)
     end_all(sum_sub, 1, N_SUB)
 
 
@@ -447,16 +432,16 @@
     scratch = [
         vm((SUBDOMS, ORDER, ORDER), BF16),
         vm((ALL, BLOCK, BLOCK), BF16),
-        vm(faces_half, F32),
         vm((COARSE, COARSE), F32),
         vm(faces_half, BF16),
-        vm(faces_half, F32),
         vm(faces_half, BF16),
         vm(faces_half, BF16),
         vm(slots_half, BF16),
         vm(slots_half, BF16),
         vm(slots_half, BF16),
+        vm(slots_half, F32),
         vm(faces_half, BF16),
+        vm((SLOTS - UP, BLOCK, COLS), BF16),
         vm((UP, BLOCK, COLS), BF16),
         vm((UP, BLOCK, COLS), BF16),
         vm((SLOTS - UP, BLOCK, COLS), BF16),
@@ -476,14 +461,14 @@
         dma((2, 3, N_GRP - 1)), dma((2, 3, N_GRP - 1)),
         dma((2, N_SUB - 1)), dma((2, N_SUB - 1)),
     ]
-    out = pl.pallas_call(
+    loads, residual, coef = pl.pallas_call(
         kernel,
-        out_shape=pltpu.VMEM(faces_half, F32),
+        out_shape=[vm(faces_half, F32), vm(faces_half, F32), vm((8, COLS), F32)],
         in_specs=[anywhere] * 4 + [scalar] * 2,
-        out_specs=pl.BlockSpec(memory_space=pltpu.VMEM),
+        out_specs=[pl.BlockSpec(memory_space=pltpu.VMEM)] * 3,
         scratch_shapes=scratch,
         compiler_params=pltpu.CompilerParams(
-            collective_id=0, has_side_effects=True, vmem_limit_bytes=50 * 1024 * 1024
+            collective_id=0, has_side_effects=True, vmem_limit_bytes=46 * 1024 * 1024
         ),
     )(
         schur,
@@ -493,6 +478,7 @@
         partner,
         corner_map,
     )
+    out = coef[0] * loads + coef[1] * residual
     return out.reshape(SUBDOMS, ORDER, COLS)
 
 

time: 64.1 us -> 61.3 us (0.956)
  Pallas kernels: 61.2 us -> 56.9 us
  other arithmetic: 0 us -> 4.2 us
  local copies, waits for them, and re-layouts: 2.71 us -> 0.02 us
    pallas_call x1, Pallas kernels: 61.2 us -> 56.9 us  [on_device(): pl.pallas_call(kernel, out_shape=[vm(faces_half, F32), vm(faces_half, F32...]
    add x0 -> x1, other arithmetic: none -> 4.2 us  [on_device(): out = coef[0] * loads + coef[1] * residual]
    unnamed x1 -> x0, local copies, waits for them, and re-layouts: 2.71 us -> none
where the time goes in v3:
time: 61.3 us; the launch traced here: 61.2 us
  Pallas kernels  56.9 us (93%)
  other arithmetic  4.2 us (7%)
    pallas_call x1, Pallas kernels, on_device(): pl.pallas_call(kernel, out_shape=[vm(faces_half, F32), vm(faces_half, F32...  56.9 us
    add x1, other arithmetic, on_device(): out = coef[0] * loads + coef[1] * residual  4.2 us

profile of v3, /device:TPU:1, one launch (start us, length us, event | category | flops | bytes accessed | tf_op | source)
XLA Modules:
  0.0 61.2 jit_solution(11477065113491047498)
XLA Ops:
  0.0 56.9 %shard_map.64 = (f32[32,128,384]{2,1,0:T(8,128)S(1)}, f32[32,128,384]{2,1,0:T(8,128)S(1)}, f32[8,384]{1,0:T(8,128)S(1)}) custom-call(bf16[4,1024,1024]{2,1,0:T(8,128)(2,1)} %schur_h.1, bf16[32,128,128]{2,1,0:T(8,128)(2,1)} %bitcast.4, f32[32,128,384]{2,1,0:T(8,128)} %bitcast.3, f32[1,128,128]{2,1,0:T(8,128)} %coarse_h.1, s32[4,4]{1,0:T(4,128)} %partner.1, ...), custom_call_target="tpu_custom_call" | custom-call | tf_op jit(solution)/shard_map/pallas_call | solution.py:464
  57.0 4.2 %multiply_add_fusion = f32[32,128,384]{2,1,0:T(8,128)} fusion(f32[32,128,384]{2,1,0:T(8,128)S(1)} %get-tuple-element.10, f32[32,128,384]{2,1,0:T(8,128)S(1)} %get-tuple-element.9, f32[384]{0:T(512)S(1)} %get-tuple-element.12, f32[384]{0:T(512)S(1)} %get-tuple-element.11), kind=kLoop, calls=%fused_computation | loop fusion | flops 4718592 | bytes 18877440 | tf_op jit(solution)/shard_map/add | solution.py:481
  (1 shorter events, 0.0 us)

commit v4 on v3

--- a/solution.py
+++ b/solution.py
@@ -42,8 +42,8 @@
 
 
 def kernel(
-    schur_h, mortar_h, load_h, coarse_h, partner, cmap, B, Q, COEF,
-    S, M, K, VB, RB, TR, SU, AB, MT, PP, TQ, TU, SU2, RU2, RD2,
+    schur_h, mortar_h, load_h, coarse_h, partner, cmap, Q,
+    S, M, B, K, VB, RB, TR, SU, AB, MT, PP, TQ, TU, SU2, RU2, RD2,
     OH, CR, CA, CX, RX, GX, AS, AG, AZ, INV,
     load_s, mort_s, schur_s, coarse_s,
     sd_s, sd_r, su_s, su_r, td_s, td_r, tu_s, tu_r,
@@ -354,21 +354,24 @@
     acc_n, acc_g = lax.fori_loop(0, SUBDOMS, resid, (zero8, zero8))
 
     def inner(s, acc):
-        field = RB[s * FACES : (s + 1) * FACES].reshape(ORDER, COLS)
-
-        def tile(i, acc):
-            part = mul(S[s, pl.ds(pl.multiple_of(i * TILE, TILE), TILE), :], field)
-            for t in range(PER):
-                acc = acc + rows8(Q[s * FACES + i * PER + t] * part[t * BLOCK : (t + 1) * BLOCK])
-            return acc
-
-        return lax.fori_loop(0, ORDER // TILE, tile, acc)
+        for half in range(2):
+            at = s * FACES + half * HALF
+            own = RB[at : at + HALF].reshape(ORDER // 2, COLS)
+            rows = pl.ds(half * (ORDER // 2), ORDER // 2)
+            part = mul(S[s, rows, rows], own * jnp.asarray(0.5, BF16))
+            if half == 0:
+                other = RB[at + HALF : at + FACES].reshape(ORDER // 2, COLS)
+                part = part + mul(S[s, rows, pl.ds(ORDER // 2, ORDER // 2)], other)
+            for t in range(HALF):
+                acc = acc + rows8(Q[at + t] * part[t * BLOCK : (t + 1) * BLOCK])
+        return acc
 
     energy = inner(0, zero8)
     energy = inner(1, energy)
     coarse_middle(1)
     energy = inner(2, energy)
     energy = inner(3, energy)
+    energy = energy + energy
 
     def pair2(first_jump, own, mate):
         d = first_jump.astype(F32) - step0 * (own.astype(F32) - mate.astype(F32))
@@ -417,9 +420,12 @@
     step1 = norm1 / curve1
     with_load = step0 + step1 * beta
 
-    COEF[0:1, :] = with_load
-    COEF[1:2, :] = step1
-    COEF[2:8, :] = jnp.zeros((6, COLS), F32)
+    @pl.loop(0, SUBDOMS)
+    def _(s):
+        for f in range(FACES):
+            g = s * FACES + f
+            Q[g] = with_load * B[g] + step1 * Q[g]
+
     end_all(sum_sub, 1, N_SUB)
 
 
@@ -432,6 +438,7 @@
     scratch = [
         vm((SUBDOMS, ORDER, ORDER), BF16),
         vm((ALL, BLOCK, BLOCK), BF16),
+        vm(faces_half, F32),
         vm((COARSE, COARSE), F32),
         vm(faces_half, BF16),
         vm(faces_half, BF16),
@@ -461,14 +468,14 @@
         dma((2, 3, N_GRP - 1)), dma((2, 3, N_GRP - 1)),
         dma((2, N_SUB - 1)), dma((2, N_SUB - 1)),
     ]
-    loads, residual, coef = pl.pallas_call(
+    out = pl.pallas_call(
         kernel,
-        out_shape=[vm(faces_half, F32), vm(faces_half, F32), vm((8, COLS), F32)],
+        out_shape=vm(faces_half, F32),
         in_specs=[anywhere] * 4 + [scalar] * 2,
-        out_specs=[pl.BlockSpec(memory_space=pltpu.VMEM)] * 3,
+        out_specs=pl.BlockSpec(memory_space=pltpu.VMEM),
         scratch_shapes=scratch,
         compiler_params=pltpu.CompilerParams(
-            collective_id=0, has_side_effects=True, vmem_limit_bytes=46 * 1024 * 1024
+            collective_id=0, has_side_effects=True, vmem_limit_bytes=52 * 1024 * 1024
         ),
     )(
         schur,
@@ -478,7 +485,6 @@
         partner,
         corner_map,
     )
-    out = coef[0] * loads + coef[1] * residual
     return out.reshape(SUBDOMS, ORDER, COLS)
 
 

time: 61.3 us -> 59.3 us (0.967)
  other arithmetic: 4.2 us -> 0 us
  local copies, waits for them, and re-layouts: 0.02 us -> 2.71 us
    add x1 -> x0, other arithmetic: 4.2 us -> none  [on_device(): out = coef[0] * loads + coef[1] * residual]
    unnamed x0 -> x1, local copies, waits for them, and re-layouts: none -> 2.71 us
where the time goes in v4:
time: 59.3 us; the launch traced here: 59.2 us
  Pallas kernels  56.5 us (95%)
  local copies, waits for them, and re-layouts  2.71 us (5%)
    pallas_call x1, Pallas kernels, on_device(): pl.pallas_call(kernel, out_shape=vm(faces_half, F32), in_specs=[anywhere]...  56.5 us
    unnamed x1, local copies, waits for them, and re-layouts  2.71 us

profile of v4, /device:TPU:1, one launch (start us, length us, event | category | flops | bytes accessed | tf_op | source)
XLA Modules:
  0.0 59.2 jit_solution(17572352696175139511)
XLA Ops:
  0.0 56.5 %shard_map.64 = f32[32,128,384]{2,1,0:T(8,128)S(1)} custom-call(bf16[4,1024,1024]{2,1,0:T(8,128)(2,1)} %schur_h.1, bf16[32,128,128]{2,1,0:T(8,128)(2,1)} %bitcast.5, f32[32,128,384]{2,1,0:T(8,128)} %bitcast.4, f32[1,128,128]{2,1,0:T(8,128)} %coarse_h.1, s32[4,4]{1,0:T(4,128)} %partner.1, s32[4,8]{1,0:T(4,128)} %cmap.1), custom_call_target="tpu_custom_call" | custom-call | tf_op jit(solution)/shard_map/pallas_call | solution.py:471
  56.5 2.7 %copy.8 = f32[4,1024,384]{2,1,0:T(8,128)} copy(f32[4,1024,384]{2,1,0:T(8,128)S(1)} %bitcast.3) | data formatting | bytes 12582912
